TPU v7x, 32 devices: a whole 2x2x4 slice. The times are simulated.
32 devices in a mesh: row: 2 (over x), col: 16 (over z, y, core).
Axes of the slice: x: 2, y: 2, z: 4, core: 2. Of those that a mesh axis runs over, the one named last changes fastest.
Arguments:
- coords: float32 [64, 3, 256], P(('row', 'col')), may hold values from 0 to 8, as said below
- noise_var: float32 [64, 256], P(('row', 'col')), may hold values from 0.1 to 1
- right_side: float32 [64, 8, 256], P(('row', 'col')), may hold values from -32 to 32
- start_guess: float32 [64, 8, 256], P(('row', 'col')), may hold values from -3 to 3
- tile_pairs: int32 [2, 16, 2, 63], P('row', 'col'), may hold values from -1 to 31, as said below
Outputs:
- solution_field: float32 [64, 8, 256], P(('row', 'col'))
- residual: float32 [64, 8, 256], P(('row', 'col'))
Inputs may be any that keep to these rules, and one draw needn't show every extreme that they name: `coords`: each tile's points lie within one unit cell of the integer lattice, and distinct tiles lie in distinct cells. `tile_pairs`: each device's list holds every pair of its block whose cells differ by at most one in each coordinate, each pair once and no other; listed entries come first, then entries of -1 in both rows.
All inputs are finite; a program needn't handle non-finite values.
Results may differ from a plain program's by a relative error of at most 0.0003.
Values sent between devices are 32-bit elements; how exact they have to be, the bound alone decides.
A program may use at most 64 MiB of HBM per device.

v0:
```python
import jax
import jax.numpy as jnp
from jax import lax
from jax.sharding import PartitionSpec as P

ITERS = 3
pair_group = 2


def wendland(left_points, right_points):
    squared = jnp.zeros(
        (left_points.shape[0], left_points.shape[2], right_points.shape[2]), jnp.float32
    )
    for component in range(3):
        spacing = left_points[:, component, :, None] - right_points[:, component, None, :]
        squared = squared + spacing * spacing
    distance = jnp.sqrt(squared)
    remain = jnp.maximum(1.0 - distance, 0.0)
    return remain**4 * (4.0 * distance + 1.0)


def squares(residual):
    return lax.psum(jnp.sum(residual * residual, axis=(0, 2)), ("row", "col"))


def shards(coords, noise_var, right_side, start_guess, tile_pairs):
    row_points = lax.all_gather(coords, "col", axis=0, tiled=True)
    col_points = lax.all_gather(coords, "row", axis=0, tiled=True)
    row_count = row_points.shape[0]
    listed = tile_pairs[0, 0]
    usable = listed[0] >= 0
    sort_key = jnp.where(usable, listed[0], row_count)
    sorted_index = jnp.argsort(sort_key, stable=True)
    sorted_rows = jnp.concatenate(
        [sort_key[sorted_index], jnp.full((pair_group,), row_count, jnp.int32)]
    )
    sorted_cols = jnp.concatenate(
        [jnp.where(usable, listed[1], 0)[sorted_index], jnp.zeros((pair_group,), jnp.int32)]
    )

    def pair_range(first_row, row_number):
        first = jnp.sum(sorted_rows < first_row)
        last = jnp.sum(sorted_rows < first_row + row_number)
        return (first, last, (last - first + pair_group - 1) // pair_group)

    def group_weights(position, last):
        indices = position + jnp.arange(pair_group, dtype=jnp.int32)
        rows_group = lax.dynamic_slice_in_dim(sorted_rows, position, pair_group)
        cols_group = lax.dynamic_slice_in_dim(sorted_cols, position, pair_group)
        inside = (indices < last).astype(jnp.float32)
        safe_rows = jnp.minimum(rows_group, row_count - 1)
        weights = wendland(row_points[safe_rows], col_points[cols_group]) * inside[:, None, None]
        return (weights, safe_rows, cols_group)

    def apply_operator(vectors):
        empty = jnp.zeros((col_points.shape[0],) + vectors.shape[1:], jnp.float32)
        pieces = lax.all_gather(vectors, "col", axis=0, tiled=True)
        number = pieces.shape[0]
        first, last, turns = pair_range(jnp.int32(0), number)

        def visit(turn, running):
            weights, safe_rows, cols_group = group_weights(first + pair_group * turn, last)
            local_rows = jnp.clip(safe_rows, 0, number - 1)
            product = jnp.einsum(
                "pab,psa->psb", weights, pieces[local_rows], precision=lax.Precision.HIGHEST
            )
            return running.at[cols_group].add(product)

        gathered_sum = lax.fori_loop(0, turns, visit, empty)
        coupled = lax.psum_scatter(gathered_sum, "row", scatter_dimension=0, tiled=True)
        return coupled + noise_var[:, None, :] * vectors

    solution_field = start_guess
    residual = right_side - apply_operator(start_guess)
    direction = residual
    norm_now = squares(residual)
    for iteration in range(ITERS):
        applied = apply_operator(direction)
        step_size = norm_now / lax.psum(jnp.sum(direction * applied, axis=(0, 2)), ("row", "col"))
        solution_field = solution_field + step_size[None, :, None] * direction
        residual = residual - step_size[None, :, None] * applied
        norm_next = squares(residual)
        direction = residual + (norm_next / norm_now)[None, :, None] * direction
        norm_now = norm_next
    return (solution_field, residual)


def solution(mesh):
    placed = (
        P(("row", "col"), None, None),
        P(("row", "col"), None),
        P(("row", "col"), None, None),
        P(("row", "col"), None, None),
        P("row", "col", None, None),
    )
    return jax.shard_map(
        shards,
        mesh=mesh,
        in_specs=placed,
        out_specs=(P(("row", "col"), None, None), P(("row", "col"), None, None)),
        check_vma=False,
    )
```

profile of v0, /device:TPU:0, one launch (start us, length us, event | category | flops | bytes accessed | tf_op | source)
XLA Modules:
  0.0 646.0 jit_solution(4284149621219089081)
XLA Ops:
  8.0 2.0 sort.17
  13.5 23.5 %all_gather.19 = f32[32,3,256]{2,1,0:T(4,128)S(1)} all-gather(f32[2,3,256]{2,1,0:T(4,128)S(1)} %copy.11), channel_id=1, replica_groups=mesh['row'=2,'col'=16] {'col'}, dimensions={0}, use_global_device_ids=true | all-gather | bytes 104448 | tf_op jit(solution)/shard_map/all_gather | solution.py:27
  36.9 4.3 all_gather.20
  42.1 17.8 %all_gather.18 = f32[32,8,256]{2,1,0:T(8,128)S(1)} all-gather(f32[2,8,256]{2,1,0:T(8,128)S(1)} %copy-done.5), channel_id=1, replica_groups=mesh['row'=2,'col'=16] {'col'}, dimensions={0}, use_global_device_ids=true | all-gather | bytes 278528 | tf_op jit(solution)/shard_map/all_gather | solution.py:57
  59.9 55.7 %while.40 = (s32[]{:T(128)}, f32[4,8,256]{2,1,0:T(8,128)S(1)}, s32[]{:T(128)}, s32[]{:T(128)}, s32[65]{0:T(128)S(1)}, /*index=5*/s32[65]{0:T(128)S(1)}, f32[32,8...) while((s32[]{:T(128)}, f32[4,8,256]{2,1,0:T(8,128)S(1)}, ...), condition=%wide.region_5.6_spmd, body=%wide.region_3.5_spmd.sunk | while | flops 14687269 | bytes 213307 | solution.py:69
  116.3 22.8 %reduce-scatter.5.cloned.1.call-done = f32[2,8,256]{2,1,0:T(8,128)} async-done(((f32[4,8,256]{2,1,0:T(8,128)}), f32[2,8,256]{2,1,0:T(8,128)}) %reduce-scatter.5.cloned.1.call-update) | async-done | bytes 16400 | tf_op jit(solution)/shard_map/reduce_scatter | solution.py:70
  139.9 22.0 %all_gather.21 = f32[32,8,256]{2,1,0:T(8,128)S(1)} all-gather(f32[2,8,256]{2,1,0:T(8,128)S(1)} %add_subtract_fusion), channel_id=1, replica_groups=mesh['row'=2,'col'=16] {'col'}, dimensions={0}, use_global_device_ids=true | all-gather | bytes 278528 | tf_op jit(solution)/shard_map/all_gather | solution.py:57
  161.9 55.7 %while.41 = (s32[]{:T(128)}, f32[4,8,256]{2,1,0:T(8,128)S(1)}, s32[]{:T(128)}, s32[]{:T(128)}, s32[65]{0:T(128)S(1)}, /*index=5*/s32[65]{0:T(128)S(1)}, f32[32,8...) while((s32[]{:T(128)}, f32[4,8,256]{2,1,0:T(8,128)S(1)}, ...), condition=%wide.region_11.12_spmd, body=%wide.region_9.11_spmd.sunk | while | flops 14687269 | bytes 213307 | solution.py:69
  179.0 0.8 fusion.167
  218.3 20.3 %reduce-scatter.7.cloned.1.call-done = f32[2,8,256]{2,1,0:T(8,128)} async-done(((f32[4,8,256]{2,1,0:T(8,128)}), f32[2,8,256]{2,1,0:T(8,128)}) %reduce-scatter.7.cloned.1.call-update) | async-done | bytes 16400 | tf_op jit(solution)/shard_map/reduce_scatter | solution.py:70
  238.6 0.9 multiply_reduce_fusion.4
  239.5 39.3 %all-reduce.2 = (f32[8]{0:T(128)S(1)}, f32[8]{0:T(128)S(1)}) all-reduce(f32[8]{0:T(128)S(1)} %get-tuple-element.221, f32[8]{0:T(128)S(1)} %get-tuple-element.220), channel_id=1, replica_groups=mesh['row'=2,'col'=16] {'row','col'}, use_global_device_ids=true, to_apply=%region_8.9 | all-reduce | flops 16 | bytes 128 | tf_op jit(solution)/shard_map/psum | solution.py:23
  279.1 40.9 %psum.44 = f32[8]{0:T(128)S(1)} all-reduce(f32[8]{0:T(128)S(1)} %multiply_reduce_fusion.3), channel_id=1, replica_groups=mesh['row'=2,'col'=16] {'row','col'}, use_global_device_ids=true, to_apply=%region_16.17 | all-reduce | flops 8 | bytes 64 | tf_op jit(solution)/shard_map/psum | solution.py:23
  320.1 21.8 %all_gather.22 = f32[32,8,256]{2,1,0:T(8,128)S(1)} all-gather(f32[2,8,256]{2,1,0:T(8,128)S(1)} %multiply_add_fusion.4), channel_id=1, replica_groups=mesh['row'=2,'col'=16] {'col'}, dimensions={0}, use_global_device_ids=true | all-gather | bytes 278528 | tf_op jit(solution)/shard_map/all_gather | solution.py:57
  341.9 55.7 %while.42 = (s32[]{:T(128)}, f32[4,8,256]{2,1,0:T(8,128)S(1)}, s32[]{:T(128)}, s32[]{:T(128)}, s32[65]{0:T(128)S(1)}, /*index=5*/s32[65]{0:T(128)S(1)}, f32[32,8...) while((s32[]{:T(128)}, f32[4,8,256]{2,1,0:T(8,128)S(1)}, ...), condition=%wide.region_19.20_spmd, body=%wide.region_17.19_spmd.sunk | while | flops 14687269 | bytes 213307 | solution.py:69
  398.3 20.3 %reduce-scatter.9.cloned.1.call-done = f32[2,8,256]{2,1,0:T(8,128)} async-done(((f32[4,8,256]{2,1,0:T(8,128)}), f32[2,8,256]{2,1,0:T(8,128)}) %reduce-scatter.9.cloned.1.call-update) | async-done | bytes 16400 | tf_op jit(solution)/shard_map/reduce_scatter | solution.py:70
  418.6 0.9 multiply_reduce_fusion.2
  419.5 39.3 %psum.45 = f32[8]{0:T(128)S(1)} all-reduce(f32[8]{0:T(128)S(1)} %multiply_reduce_fusion.2), channel_id=1, replica_groups=mesh['row'=2,'col'=16] {'row','col'}, use_global_device_ids=true, to_apply=%region_22.23 | all-reduce | flops 8 | bytes 64 | tf_op jit(solution)/shard_map/psum | solution.py:79
  459.0 41.0 %psum.46 = f32[8]{0:T(128)S(1)} all-reduce(f32[8]{0:T(128)S(1)} %get-tuple-element.306), channel_id=1, replica_groups=mesh['row'=2,'col'=16] {'row','col'}, use_global_device_ids=true, to_apply=%region_24.25 | all-reduce | flops 8 | bytes 64 | tf_op jit(solution)/shard_map/psum | solution.py:23
  500.1 21.8 %all_gather.23 = f32[32,8,256]{2,1,0:T(8,128)S(1)} all-gather(f32[2,8,256]{2,1,0:T(8,128)S(1)} %multiply_add_fusion.2), channel_id=1, replica_groups=mesh['row'=2,'col'=16] {'col'}, dimensions={0}, use_global_device_ids=true | all-gather | bytes 278528 | tf_op jit(solution)/shard_map/all_gather | solution.py:57
  521.9 55.7 %while.43 = (s32[]{:T(128)}, f32[4,8,256]{2,1,0:T(8,128)S(1)}, s32[]{:T(128)}, s32[]{:T(128)}, s32[65]{0:T(128)S(1)}, /*index=5*/s32[65]{0:T(128)S(1)}, f32[32,8...) while((s32[]{:T(128)}, f32[4,8,256]{2,1,0:T(8,128)S(1)}, ...), condition=%wide.region_27.28_spmd, body=%wide.region_25.27_spmd.sunk | while | flops 14687269 | bytes 213307 | solution.py:69
  578.3 20.3 %reduce-scatter.11.cloned.1.call-done = f32[2,8,256]{2,1,0:T(8,128)} async-done(((f32[4,8,256]{2,1,0:T(8,128)}), f32[2,8,256]{2,1,0:T(8,128)}) %reduce-scatter.11.cloned.1.call-update) | async-done | bytes 16400 | tf_op jit(solution)/shard_map/reduce_scatter | solution.py:70
  598.6 0.9 multiply_reduce_fusion
  599.5 39.3 %psum.47 = f32[8]{0:T(128)S(1)} all-reduce(f32[8]{0:T(128)S(1)} %multiply_reduce_fusion), channel_id=1, replica_groups=mesh['row'=2,'col'=16] {'row','col'}, use_global_device_ids=true, to_apply=%region_30.31 | all-reduce | flops 8 | bytes 64 | tf_op jit(solution)/shard_map/psum | solution.py:79
  (917 shorter events, 194.2 us)
Async XLA Ops:
  7.2 132.0 %reduce-scatter.5.cloned.1.call-start = ((), (), s32[]{:S(2)}) async-start(), calls=%async_computation.4 | async-start | bytes 49152 | tf_op jit(solution)/shard_map/reduce_scatter | solution.py:70
  12.8 0.7 copy-start.10
  41.3 0.8 copy-start.5
  115.7 0.6 copy-start.1
  115.7 23.5 %copy-start.6 = (f32[2,256]{1,0:T(2,128)S(1)}, f32[2,256]{1,0:T(2,128)}, u32[]{:S(2)}) copy-start(f32[2,256]{1,0:T(2,128)} %param.14) | copy-start | bytes 6148
  115.7 23.5 %copy-start.9 = (f32[2,8,256]{2,1,0:T(8,128)S(1)}, f32[2,8,256]{2,1,0:T(8,128)}, u32[]{:S(2)}) copy-start(f32[2,8,256]{2,1,0:T(8,128)} %param.15) | copy-start | bytes 49156
  116.3 122.3 %reduce-scatter.7.cloned.1.call-start = ((), (), s32[]{:S(2)}) async-start(), calls=%async_computation.5 | async-start | bytes 49152 | tf_op jit(solution)/shard_map/reduce_scatter | solution.py:70
  217.6 0.6 copy-start.2
  218.2 200.4 %reduce-scatter.9.cloned.1.call-start = ((), (), s32[]{:S(2)}) async-start(), calls=%async_computation.6 | async-start | bytes 49152 | tf_op jit(solution)/shard_map/reduce_scatter | solution.py:70
  238.6 40.3 %copy-start.4 = (f32[2,8,256]{2,1,0:T(8,128)S(1)}, f32[2,8,256]{2,1,0:T(8,128)}, u32[]{:S(2)}) copy-start(f32[2,8,256]{2,1,0:T(8,128)} %reduce-scatter.7.cloned.1.call-done) | copy-start | bytes 49156
  397.6 0.6 copy-start.3
  398.3 200.3 %reduce-scatter.11.cloned.1.call-start = ((), (), s32[]{:S(2)}) async-start(), calls=%async_computation.7 | async-start | bytes 49152 | tf_op jit(solution)/shard_map/reduce_scatter | solution.py:70
  418.6 40.2 %copy-start.8 = (f32[2,8,256]{2,1,0:T(8,128)S(1)}, f32[2,8,256]{2,1,0:T(8,128)}, u32[]{:S(2)}) copy-start(f32[2,8,256]{2,1,0:T(8,128)} %reduce-scatter.9.cloned.1.call-done) | copy-start | bytes 49156
  577.6 0.6 copy-start
  598.6 40.2 %copy-start.7 = (f32[2,8,256]{2,1,0:T(8,128)S(1)}, f32[2,8,256]{2,1,0:T(8,128)}, u32[]{:S(2)}) copy-start(f32[2,8,256]{2,1,0:T(8,128)} %reduce-scatter.11.cloned.1.call-done) | copy-start | bytes 49156
Sparse Core Ops, SparseCore 0:
  116.4 22.6 reduce-scatter.4
  218.4 20.1 reduce-scatter.6
  398.4 20.1 reduce-scatter.8
  578.4 20.1 reduce-scatter.10
where the time goes:
time: 649 us; the launch traced here: 646 us
  blocking collectives  311 us (48%)
  local copies, waits for them, and re-layouts  87.6 us (13%)
  waiting for transfers between devices  83.8 us (13%)
  other arithmetic  72.8 us (11%)
  matrix products  39.1 us (6%)
  loops' own time  36.2 us (6%)
  between operations  15.2 us (2%)
    psum x3, blocking collectives, squares(): return lax.psum(jnp.sum(residual * residual, axis=(0, 2)), ('row', 'col'))  121 us
    reduce_scatter x4, waiting for transfers between devices, apply_operator(): lax.psum_scatter(gathered_sum, 'row', scatter_dimension=0, tiled=True)  83.7 us
    all_gather x4, blocking collectives, apply_operator(): pieces = lax.all_gather(vectors, 'col', axis=0, tiled=True)  83.5 us
    psum x2, blocking collectives, shards(): lax.psum(jnp.sum(direction * applied, axis=(0, 2)), ('row', 'col'))  78.6 us
    dot_general x48, matrix products, visit(): jnp.einsum('pab,psa->psb', weights, pieces[local_rows], precision=lax.Pre...  39.1 us
    another operation x4, loops' own time, apply_operator(): gathered_sum = lax.fori_loop(0, turns, visit, empty)  36.2 us
    convert_element_type x48, other arithmetic, group_weights(): inside = (indices < last).astype(jnp.float32)  30.5 us
    scatter-add x48, other arithmetic, visit(): return running.at[cols_group].add(product)  29.3 us
  transfers between devices with their start and end apart: 4, of which 4 were waited for; matrix products, arithmetic and copies ran while one was open for 0% of the time, Pallas kernels for 0%

commit v1 on v0

--- a/solution.py
+++ b/solution.py
@@ -20,7 +20,7 @@
 
 
 def squares(residual):
-    return lax.psum(jnp.sum(residual * residual, axis=(0, 2)), ("row", "col"))
+    return lax.psum(lax.psum(jnp.sum(residual * residual, axis=(0, 2)), "col"), "row")
 
 
 def shards(coords, noise_var, right_side, start_guess, tile_pairs):

time: 649 us -> 671 us (1.034)
  blocking collectives: 311 us -> 329 us
    psum x2 -> x3, blocking collectives: 78.6 us -> 115 us  [shards(): lax.psum(jnp.sum(direction * applied, axis=(0, 2)), ('row', 'col'))]
    psum x3 -> x6, blocking collectives: 121 us -> 111 us  [the longest x3 95.9 us: squares(): lax.psum(jnp.sum(residual * residual, axis=(0, 2)), 'col')]
    all_gather x4, blocking collectives: 83.5 us -> 75.5 us  [apply_operator(): pieces = lax.all_gather(vectors, 'col', axis=0, tiled=True)]
where the time goes in v1:
time: 671 us; the launch traced here: 668 us
  blocking collectives  329 us (49%)
  waiting for transfers between devices  87.9 us (13%)
  local copies, waits for them, and re-layouts  87.6 us (13%)
  other arithmetic  72.8 us (11%)
  matrix products  39.1 us (6%)
  loops' own time  36.2 us (5%)
  between operations  15.2 us (2%)
    psum x3, blocking collectives, shards(): lax.psum(jnp.sum(direction * applied, axis=(0, 2)), ('row', 'col'))  115 us
    psum x3, blocking collectives, squares(): lax.psum(jnp.sum(residual * residual, axis=(0, 2)), 'col')  95.9 us
    reduce_scatter x4, waiting for transfers between devices, apply_operator(): lax.psum_scatter(gathered_sum, 'row', scatter_dimension=0, tiled=True)  87.9 us
    all_gather x4, blocking collectives, apply_operator(): pieces = lax.all_gather(vectors, 'col', axis=0, tiled=True)  75.5 us
    dot_general x48, matrix products, visit(): jnp.einsum('pab,psa->psb', weights, pieces[local_rows], precision=lax.Pre...  39.1 us
    another operation x4, loops' own time, apply_operator(): gathered_sum = lax.fori_loop(0, turns, visit, empty)  36.2 us
    convert_element_type x48, other arithmetic, group_weights(): inside = (indices < last).astype(jnp.float32)  30.5 us
    scatter-add x48, other arithmetic, visit(): return running.at[cols_group].add(product)  29.3 us
  transfers between devices with their start and end apart: 4, of which 4 were waited for; matrix products, arithmetic and copies ran while one was open for 0% of the time, Pallas kernels for 0%

profile of v1, /device:TPU:0, one launch (start us, length us, event | category | flops | bytes accessed | tf_op | source)
XLA Modules:
  0.0 668.3 jit_solution(10248715553529206802)
XLA Ops:
  8.0 2.0 sort.17
  13.5 23.5 %all_gather.19 = f32[32,3,256]{2,1,0:T(4,128)S(1)} all-gather(f32[2,3,256]{2,1,0:T(4,128)S(1)} %copy.11), channel_id=1, replica_groups=mesh['row'=2,'col'=16] {'col'}, dimensions={0}, use_global_device_ids=true | all-gather | bytes 104448 | tf_op jit(solution)/shard_map/all_gather | solution.py:27
  36.9 4.3 all_gather.20
  42.1 17.8 %all_gather.18 = f32[32,8,256]{2,1,0:T(8,128)S(1)} all-gather(f32[2,8,256]{2,1,0:T(8,128)S(1)} %copy-done.5), channel_id=1, replica_groups=mesh['row'=2,'col'=16] {'col'}, dimensions={0}, use_global_device_ids=true | all-gather | bytes 278528 | tf_op jit(solution)/shard_map/all_gather | solution.py:57
  59.9 55.7 %while.40 = (s32[]{:T(128)}, f32[4,8,256]{2,1,0:T(8,128)S(1)}, s32[]{:T(128)}, s32[]{:T(128)}, s32[65]{0:T(128)S(1)}, /*index=5*/s32[65]{0:T(128)S(1)}, f32[32,8...) while((s32[]{:T(128)}, f32[4,8,256]{2,1,0:T(8,128)S(1)}, ...), condition=%wide.region_5.6_spmd, body=%wide.region_3.5_spmd.sunk | while | flops 14687269 | bytes 213307 | solution.py:69
  116.3 22.8 %reduce-scatter.5.cloned.1.call-done = f32[2,8,256]{2,1,0:T(8,128)} async-done(((f32[4,8,256]{2,1,0:T(8,128)}), f32[2,8,256]{2,1,0:T(8,128)}) %reduce-scatter.5.cloned.1.call-update) | async-done | bytes 16400 | tf_op jit(solution)/shard_map/reduce_scatter | solution.py:70
  139.9 22.0 %all_gather.21 = f32[32,8,256]{2,1,0:T(8,128)S(1)} all-gather(f32[2,8,256]{2,1,0:T(8,128)S(1)} %add_subtract_fusion), channel_id=1, replica_groups=mesh['row'=2,'col'=16] {'col'}, dimensions={0}, use_global_device_ids=true | all-gather | bytes 278528 | tf_op jit(solution)/shard_map/all_gather | solution.py:57
  161.9 55.7 %while.41 = (s32[]{:T(128)}, f32[4,8,256]{2,1,0:T(8,128)S(1)}, s32[]{:T(128)}, s32[]{:T(128)}, s32[65]{0:T(128)S(1)}, /*index=5*/s32[65]{0:T(128)S(1)}, f32[32,8...) while((s32[]{:T(128)}, f32[4,8,256]{2,1,0:T(8,128)S(1)}, ...), condition=%wide.region_12.13_spmd, body=%wide.region_10.12_spmd.sunk | while | flops 14687269 | bytes 213307 | solution.py:69
  218.3 20.3 %reduce-scatter.7.cloned.1.call-done = f32[2,8,256]{2,1,0:T(8,128)} async-done(((f32[4,8,256]{2,1,0:T(8,128)}), f32[2,8,256]{2,1,0:T(8,128)}) %reduce-scatter.7.cloned.1.call-update) | async-done | bytes 16400 | tf_op jit(solution)/shard_map/reduce_scatter | solution.py:70
  239.5 32.6 %psum.63 = f32[8]{0:T(128)S(1)} all-reduce(f32[8]{0:T(128)S(1)} %get-tuple-element.221), channel_id=1, replica_groups=mesh['row'=2,'col'=16] {'col'}, use_global_device_ids=true, to_apply=%region_8.9 | all-reduce | flops 8 | bytes 64 | tf_op jit(solution)/shard_map/psum | solution.py:23
  272.2 4.9 psum.64
  277.1 36.8 %psum.65 = f32[8]{0:T(128)S(1)} all-reduce(f32[8]{0:T(128)S(1)} %get-tuple-element.220), channel_id=1, replica_groups=mesh['row'=2,'col'=16] {'row','col'}, use_global_device_ids=true, to_apply=%region_15.16 | all-reduce | flops 8 | bytes 64 | tf_op jit(solution)/shard_map/psum | solution.py:79
  314.0 31.2 %psum.66 = f32[8]{0:T(128)S(1)} all-reduce(f32[8]{0:T(128)S(1)} %multiply_reduce_fusion.3), channel_id=1, replica_groups=mesh['row'=2,'col'=16] {'col'}, use_global_device_ids=true, to_apply=%region_17.18 | all-reduce | flops 8 | bytes 64 | tf_op jit(solution)/shard_map/psum | solution.py:23
  345.3 4.9 psum.67
  350.3 17.8 %all_gather.22 = f32[32,8,256]{2,1,0:T(8,128)S(1)} all-gather(f32[2,8,256]{2,1,0:T(8,128)S(1)} %multiply_add_fusion.4), channel_id=1, replica_groups=mesh['row'=2,'col'=16] {'col'}, dimensions={0}, use_global_device_ids=true | all-gather | bytes 278528 | tf_op jit(solution)/shard_map/all_gather | solution.py:57
  368.1 55.7 %while.42 = (s32[]{:T(128)}, f32[4,8,256]{2,1,0:T(8,128)S(1)}, s32[]{:T(128)}, s32[]{:T(128)}, s32[65]{0:T(128)S(1)}, /*index=5*/s32[65]{0:T(128)S(1)}, f32[32,8...) while((s32[]{:T(128)}, f32[4,8,256]{2,1,0:T(8,128)S(1)}, ...), condition=%wide.region_21.22_spmd, body=%wide.region_19.21_spmd.sunk | while | flops 14687269 | bytes 213307 | solution.py:69
  424.5 22.8 %reduce-scatter.9.cloned.1.call-done = f32[2,8,256]{2,1,0:T(8,128)} async-done(((f32[4,8,256]{2,1,0:T(8,128)}), f32[2,8,256]{2,1,0:T(8,128)}) %reduce-scatter.9.cloned.1.call-update) | async-done | bytes 16400 | tf_op jit(solution)/shard_map/reduce_scatter | solution.py:70
  448.2 39.3 %psum.68 = f32[8]{0:T(128)S(1)} all-reduce(f32[8]{0:T(128)S(1)} %multiply_reduce_fusion.2), channel_id=1, replica_groups=mesh['row'=2,'col'=16] {'row','col'}, use_global_device_ids=true, to_apply=%region_24.25 | all-reduce | flops 8 | bytes 64 | tf_op jit(solution)/shard_map/psum | solution.py:79
  487.7 32.1 %psum.69 = f32[8]{0:T(128)S(1)} all-reduce(f32[8]{0:T(128)S(1)} %get-tuple-element.304), channel_id=1, replica_groups=mesh['row'=2,'col'=16] {'col'}, use_global_device_ids=true, to_apply=%region_26.27 | all-reduce | flops 8 | bytes 64 | tf_op jit(solution)/shard_map/psum | solution.py:23
  519.8 4.9 psum.70
  524.8 17.8 %all_gather.23 = f32[32,8,256]{2,1,0:T(8,128)S(1)} all-gather(f32[2,8,256]{2,1,0:T(8,128)S(1)} %multiply_add_fusion.2), channel_id=1, replica_groups=mesh['row'=2,'col'=16] {'col'}, dimensions={0}, use_global_device_ids=true | all-gather | bytes 278528 | tf_op jit(solution)/shard_map/all_gather | solution.py:57
  542.6 55.7 %while.43 = (s32[]{:T(128)}, f32[4,8,256]{2,1,0:T(8,128)S(1)}, s32[]{:T(128)}, s32[]{:T(128)}, s32[65]{0:T(128)S(1)}, /*index=5*/s32[65]{0:T(128)S(1)}, f32[32,8...) while((s32[]{:T(128)}, f32[4,8,256]{2,1,0:T(8,128)S(1)}, ...), condition=%wide.region_30.31_spmd, body=%wide.region_28.30_spmd.sunk | while | flops 14687269 | bytes 213307 | solution.py:69
  598.9 22.0 %reduce-scatter.11.cloned.1.call-done = f32[2,8,256]{2,1,0:T(8,128)} async-done(((f32[4,8,256]{2,1,0:T(8,128)}), f32[2,8,256]{2,1,0:T(8,128)}) %reduce-scatter.11.cloned.1.call-update) | async-done | bytes 16400 | tf_op jit(solution)/shard_map/reduce_scatter | solution.py:70
  621.8 39.3 %psum.71 = f32[8]{0:T(128)S(1)} all-reduce(f32[8]{0:T(128)S(1)} %multiply_reduce_fusion), channel_id=1, replica_groups=mesh['row'=2,'col'=16] {'row','col'}, use_global_device_ids=true, to_apply=%region_33.34 | all-reduce | flops 8 | bytes 64 | tf_op jit(solution)/shard_map/psum | solution.py:79
  (921 shorter events, 197.7 us)
Async XLA Ops:
  7.2 132.0 %reduce-scatter.5.cloned.1.call-start = ((), (), s32[]{:S(2)}) async-start(), calls=%async_computation.4 | async-start | bytes 49152 | tf_op jit(solution)/shard_map/reduce_scatter | solution.py:70
  12.8 0.7 copy-start.10
  41.3 0.8 copy-start.5
  115.7 0.6 copy-start.1
  115.7 23.5 %copy-start.6 = (f32[2,256]{1,0:T(2,128)S(1)}, f32[2,256]{1,0:T(2,128)}, u32[]{:S(2)}) copy-start(f32[2,256]{1,0:T(2,128)} %param.14) | copy-start | bytes 6148
  115.7 23.5 %copy-start.9 = (f32[2,8,256]{2,1,0:T(8,128)S(1)}, f32[2,8,256]{2,1,0:T(8,128)}, u32[]{:S(2)}) copy-start(f32[2,8,256]{2,1,0:T(8,128)} %param.15) | copy-start | bytes 49156
  116.3 122.3 %reduce-scatter.7.cloned.1.call-start = ((), (), s32[]{:S(2)}) async-start(), calls=%async_computation.5 | async-start | bytes 49152 | tf_op jit(solution)/shard_map/reduce_scatter | solution.py:70
  217.6 0.6 copy-start.2
  218.2 229.0 %reduce-scatter.9.cloned.1.call-start = ((), (), s32[]{:S(2)}) async-start(), calls=%async_computation.6 | async-start | bytes 49152 | tf_op jit(solution)/shard_map/reduce_scatter | solution.py:70
  238.6 75.2 %copy-start.4 = (f32[2,8,256]{2,1,0:T(8,128)S(1)}, f32[2,8,256]{2,1,0:T(8,128)}, u32[]{:S(2)}) copy-start(f32[2,8,256]{2,1,0:T(8,128)} %reduce-scatter.7.cloned.1.call-done) | copy-start | bytes 49156
  423.8 0.6 copy-start.3
  424.4 196.5 %reduce-scatter.11.cloned.1.call-start = ((), (), s32[]{:S(2)}) async-start(), calls=%async_computation.7 | async-start | bytes 49152 | tf_op jit(solution)/shard_map/reduce_scatter | solution.py:70
  447.3 40.2 %copy-start.8 = (f32[2,8,256]{2,1,0:T(8,128)S(1)}, f32[2,8,256]{2,1,0:T(8,128)}, u32[]{:S(2)}) copy-start(f32[2,8,256]{2,1,0:T(8,128)} %reduce-scatter.9.cloned.1.call-done) | copy-start | bytes 49156
  598.3 0.6 copy-start
  620.9 40.2 %copy-start.7 = (f32[2,8,256]{2,1,0:T(8,128)S(1)}, f32[2,8,256]{2,1,0:T(8,128)}, u32[]{:S(2)}) copy-start(f32[2,8,256]{2,1,0:T(8,128)} %reduce-scatter.11.cloned.1.call-done) | copy-start | bytes 49156
Sparse Core Ops, SparseCore 0:
  116.4 22.6 reduce-scatter.4
  218.4 20.1 reduce-scatter.6
  424.6 22.6 reduce-scatter.8
  599.1 21.7 reduce-scatter.10
